TPU v7x, 32 devices: a whole 2x2x4 slice. The times are simulated.
32 devices in a mesh: bx: 4 (over y, x), by: 8 (over z, core).
Axes of the slice: x: 2, y: 2, z: 4, core: 2. Of those that a mesh axis runs over, the one named last changes fastest.
Arguments:
- speed_vectors: float32 [3, 6, 60, 120, 128], P(None, None, 'bx', 'by'), may hold values from -10 to 10, as said below
- bin_population: int32 [60, 120, 128], P('bx', 'by'), may hold values from 0 to 6, as said below
- spin_choice: int32 [12, 60, 120, 128], P(None, 'bx', 'by'), may hold values from 0 to 5
- approval_flags: int32 [12, 60, 120, 128], P(None, 'bx', 'by'), may hold values 0 or 1
- round_evenness: int32 [12], replicated, may hold values from 0 to 1
- grid_displacements: int32 [12], replicated, may hold values from 0 to 127
- thermostat_heat_level: float32 [12], replicated, may hold values from 0.5 to 2
Outputs:
- final_velocity: float32 [3, 6, 60, 120, 128], P(None, None, 'bx', 'by')
Inputs may be any that keep to these rules, and one draw needn't show every extreme that they name: `bin_population`: A cell's particles fill its first slots. `speed_vectors`: entries in slots at or beyond a cell's occupancy are not read.
All inputs are finite; a program needn't handle non-finite values. No bound on the sum of `approval_flags` on one device may be relied on, other than what follows from the above.
Results may differ from a plain program's by a relative error of at most 0.0003.
Values sent between devices are 32-bit elements; how exact they have to be, the bound alone decides.
A program may use at most 64 MiB of HBM per device.

v0:
```python
import functools
import math

import jax
import jax.numpy as jnp
from jax import lax
from jax.experimental import pallas as pl
from jax.experimental.pallas import tpu as pltpu
from jax.sharding import PartitionSpec as P

MESH = pl.DeviceIdType.MESH
AXES = ("bx", "by")
COS = math.cos(130.0 * math.pi / 180.0)
SIN = math.sin(130.0 * math.pi / 180.0)
EPSILON = 1e-06


def tree_sum(parts):
    parts = list(parts)
    while len(parts) > 1:
        parts = [sum(parts[i : i + 2]) for i in range(0, len(parts), 2)]
    return parts[0]


def column_sum(value):
    return jnp.sum(value, axis=0, keepdims=True)


def kernel(
    sizes,
    v_hbm,
    count_hbm,
    spin_hbm,
    flag_hbm,
    parity,
    displacement,
    heat,
    x_out,
    f_out,
    w,
    spin,
    flag_x,
    flag_y,
    flag_raw,
    count_x,
    count_y,
    p_x,
    p_y,
    p_z,
    p_tmp,
    iq_x,
    iq_y,
    rr_x,
    rr_y,
    closing,
    coupling,
    transfer,
    rows_by,
    rows_bx,
    load_sem,
    halo_send,
    halo_recv,
    by_send,
    by_recv,
    bx_send,
    bx_recv,
):
    n = sizes
    slots = v_hbm.shape[1]
    ex, ey, nz = count_hbm.shape
    extent = (ex, ey)
    rounds = spin_hbm.shape[0] // 2
    me = (lax.axis_index("bx"), lax.axis_index("by"))
    above = tuple(lax.rem(me[a] + 1, n[a]) for a in range(2))
    below = tuple(lax.rem(me[a] + n[a] - 1, n[a]) for a in range(2))
    flag = (flag_x, flag_y)
    count = (count_x, count_y)
    mom = (p_x, p_y)
    iq = (iq_x, iq_y)
    rr = (rr_x, rr_y)

    load_count = pltpu.make_async_copy(count_hbm, count_x.at[pl.ds(1, ex)], load_sem.at[0])
    load_v = [pltpu.make_async_copy(v_hbm.at[c], w.at[c], load_sem.at[1 + c]) for c in range(3)]
    load_fx = pltpu.make_async_copy(flag_hbm.at[:, 0], flag_x.at[:, pl.ds(1, ex)], load_sem.at[4])
    load_fy = pltpu.make_async_copy(flag_hbm.at[:, 1], flag_raw, load_sem.at[5])
    load_spin = pltpu.make_async_copy(spin_hbm, spin, load_sem.at[6])
    for copy in (load_count, load_v[0], load_fx, load_v[1], load_fy, load_v[2], load_spin):
        copy.start()

    barrier = pltpu.get_barrier_semaphore()
    for a in range(2):
        for step in range(1, n[a]):
            pl.semaphore_signal(
                barrier,
                inc=1,
                device_id={AXES[a]: lax.rem(me[a] + step, n[a])},
                device_id_type=MESH,
            )

    def halo(view, a, kind):
        k = 2 * (2 * kind + a)
        return [
            pltpu.make_async_remote_copy(
                src_ref=view(extent[a]),
                dst_ref=view(0),
                send_sem=halo_send.at[k],
                recv_sem=halo_recv.at[k],
                device_id={AXES[a]: above[a]},
                device_id_type=MESH,
            ),
            pltpu.make_async_remote_copy(
                src_ref=view(1),
                dst_ref=view(extent[a] + 1),
                send_sem=halo_send.at[k + 1],
                recv_sem=halo_recv.at[k + 1],
                device_id={AXES[a]: below[a]},
                device_id_type=MESH,
            ),
        ]

    halo_p = [halo(lambda i, a=a: mom[a].at[i], a, 0) for a in range(2)]
    halo_c = [halo(lambda i, a=a: count[a].at[i], a, 1) for a in range(2)]
    halo_f = [halo(lambda i, a=a: flag[a].at[:, i], a, 2) for a in range(2)]

    def start(copies):
        for copy in copies:
            copy.start()

    def finish(copies):
        for copy in copies:
            copy.wait()

    def inverse(counts):
        return 1.0 / jnp.maximum(counts.astype(jnp.float32), 1.0)

    def split_component(c, target, offset):
        def plane(i, acc):
            counts = count_x[i + 1]
            inv = iq_x[i + 1]
            values = [jnp.where(counts > s, w[c, s, i], 0.0) for s in range(slots)]
            moment = tree_sum(values)
            target[i + offset] = moment
            mean = moment * inv
            thermal = [jnp.where(counts > s, values[s] - mean, 0.0) for s in range(slots)]
            for s in range(slots):
                w[c, s, i] = thermal[s]
            heat_part = acc[0] + tree_sum([t * t for t in thermal])
            return heat_part, acc[1] + moment * mean

        zero = jnp.zeros((ey, nz), jnp.float32)
        return lax.fori_loop(0, ex, plane, (zero, zero))

    load_count.wait()
    number = jnp.zeros((ey, nz), jnp.float32)
    for i in range(1, ex + 1):
        iq_x[i] = inverse(count_x[i])
        number = number + count_x[i].astype(jnp.float32)
    load_v[0].wait()
    thermal_0, energy_x = split_component(0, p_x, 1)
    pl.semaphore_wait(barrier, n[0] + n[1] - 2)
    start(halo_p[0])
    start(halo_c[0])
    load_fx.wait()
    start(halo_f[0])
    load_v[1].wait()
    thermal_1, energy_y = split_component(1, p_tmp, 0)
    for y in range(ey):
        p_y[y + 1] = p_tmp[:, y, :]
        count_y[y + 1] = count_x[pl.ds(1, ex), y, :]
    start(halo_p[1])
    start(halo_c[1])
    load_fy.wait()

    def flags_across(r, carry):
        for y in range(ey):
            flag_y[r, y + 1] = flag_raw[r, :, y, :]
        return carry

    lax.fori_loop(0, rounds, flags_across, 0)
    start(halo_f[1])
    load_v[2].wait()
    thermal_2, energy_z = split_component(2, p_z, 0)

    def reduced_masses(a):
        finish(halo_c[a])
        e = extent[a]
        for i in range(0, e + 2):
            iq[a][i] = inverse(count[a][i])
        for b in range(e + 1):
            low = count[a][b].astype(jnp.float32)
            high = count[a][b + 1].astype(jnp.float32)
            rr[a][b] = low * high / jnp.maximum(low + high, 1.0)

    def offset_of(a, t):
        return (me[a] * extent[a] - parity[t]) & 1

    def prepare(a, r, t, shift):
        finish(halo_p[a])
        p = offset_of(a, t)
        back = lax.rem(nz - shift, nz)
        for j in range((extent[a] + 1) // 2):
            low = 2 * j + 1 - p
            high = 2 * j + 2 - p
            closing[j] = jnp.maximum(
                mom[a][low] * iq[a][low] - mom[a][high] * iq[a][high], 0.0
            )
            bits = jnp.maximum(flag[a][r, low], flag[a][r, high]).astype(jnp.float32)
            coupling[j] = pltpu.roll(bits, back, 1) * rr[a][low]

    def rotate(t, shift):
        back = lax.rem(nz - shift, nz)

        def plane(i, carry):
            kind = pltpu.roll(spin[t, i], back, 1)
            axis = kind >> 1
            sine = jnp.where((kind & 1) == 0, SIN, -SIN)
            own = [jnp.where(axis == c, 1.0, COS) for c in range(3)]
            sin = [jnp.where(axis == c, sine, 0.0) for c in range(3)]
            for s in range(slots):
                x, y, z = (w[c, s, i] for c in range(3))
                w[0, s, i] = own[0] * x + (sin[1] * z - sin[2] * y)
                w[1, s, i] = own[1] * y + (sin[2] * x - sin[0] * z)
                w[2, s, i] = own[2] * z + (sin[0] * y - sin[1] * x)
            return carry

        lax.fori_loop(0, ex, plane, 0)

    def exchange(rows, a, slot, send_sem, recv_sem):
        return [
            pltpu.make_async_remote_copy(
                src_ref=rows.at[slot, me[a]],
                dst_ref=rows.at[slot, me[a]],
                send_sem=send_sem,
                recv_sem=recv_sem,
                device_id={AXES[a]: lax.rem(me[a] + step, n[a])},
                device_id_type=MESH,
            )
            for step in range(1, n[a])
        ]

    def await_rows(rows, a, slot, send_sem, recv_sem):
        view = rows.at[slot, pl.ds(0, n[a] - 1)]
        whole = pltpu.make_async_remote_copy(
            src_ref=view,
            dst_ref=view,
            send_sem=send_sem,
            recv_sem=recv_sem,
            device_id={AXES[a]: above[a]},
            device_id_type=MESH,
        )
        whole.wait_recv()
        whole.wait_send()

    def collide(a, t, scale):
        p = offset_of(a, t)
        sign = (2 * p - 1).astype(jnp.float32)
        for j in range((extent[a] + 1) // 2):
            g = scale * closing[j]
            transfer[j] = coupling[j] * g * jnp.tanh(g)
        energy = []
        for i in range(1, extent[a] + 1):
            if i % 2 == 1:
                moved = scale * mom[a][i] + sign * transfer[(i - 1) // 2]
            else:
                moved = scale * mom[a][i] - sign * transfer[i // 2 - 1 + p]
            mom[a][i] = moved
            energy.append(moved * moved * iq[a][i])
        return column_sum(tree_sum(energy))

    load_spin.wait()
    reduced_masses(0)
    finish(halo_f[0])
    prepare(0, 0, 0, 0)
    number_row = column_sum(number)
    ones = jnp.ones((1, nz), jnp.float32)

    def step(a, r, scales, energies, shift, last_hook):
        t = 2 * r + a
        b = 1 - a
        new_energy = collide(a, t, scales[a])
        partial = new_energy + energies[b] + energies[2]
        rows_by[a, me[1]] = jnp.concatenate([partial, number_row], axis=0)
        start(exchange(rows_by, 1, a, by_send.at[a], by_recv.at[a]))
        if a == 0:

            @pl.when(r > 0)
            def _():
                start(halo_p[1])

        else:

            @pl.when(r < rounds - 1)
            def _():
                start(halo_p[0])

        rotate(t, shift)
        if a == 0:

            @pl.when(r == 0)
            def _():
                reduced_masses(1)
                finish(halo_f[1])

        await_rows(rows_by, 1, a, by_send.at[a], by_recv.at[a])
        rows_bx[a, me[0]] = tree_sum([rows_by[a, i] for i in range(n[1])])
        start(exchange(rows_bx, 0, a, bx_send.at[a], bx_recv.at[a]))
        new_shift = lax.rem(shift + displacement[t], nz)
        if a == 0:
            prepare(1, r, t + 1, new_shift)
        else:

            @pl.when(r < rounds - 1)
            def _():
                prepare(0, r + 1, t + 1, new_shift)

            @pl.when(r == rounds - 1)
            def _():
                last_hook(scales, new_shift)

        await_rows(rows_bx, 0, a, bx_send.at[a], bx_recv.at[a])
        sums = tree_sum([rows_bx[a, i] for i in range(n[0])])
        sums = jnp.sum(sums, axis=1, keepdims=True)
        square = 3.0 * heat[t] * sums[1:2] / (sums[0:1] + EPSILON)
        square = jnp.broadcast_to(square, (1, nz))
        f = jnp.sqrt(square)
        kept = scales[b] * f
        scales = (f, kept, scales[2] * f) if a == 0 else (kept, f, scales[2] * f)
        moved = new_energy * square
        other = energies[b] * square
        pair = (moved, other) if a == 0 else (other, moved)
        return scales, pair + (energies[2] * square,), new_shift, f

    def assemble(scales, shift):
        for y in range(ey):
            p_tmp[:, y, :] = p_y[y + 1]

        def plane(i, carry):
            counts = count_x[i + 1]
            inv = iq_x[i + 1]
            means = (
                scales[0] * (p_x[i + 1] * inv),
                p_tmp[i] * inv,
                scales[2] * (p_z[i] * inv),
            )
            for c in range(3):
                for s in range(slots):
                    value = jnp.where(counts > s, means[c] + scales[2] * w[c, s, i], 0.0)
                    x_out[c, s, i] = pltpu.roll(value, shift, 1)
            return carry

        lax.fori_loop(0, ex, plane, 0)

    def round_body(r, carry):
        scales, energies, shift, _ = carry
        scales, energies, shift, f = step(0, r, scales, energies, shift, None)
        return step(1, r, scales, energies, shift, assemble)

    rest = column_sum(thermal_0 + thermal_1 + thermal_2 + energy_z)
    energies = (column_sum(energy_x), column_sum(energy_y), rest)
    carry = ((ones, ones, ones), energies, jnp.int32(0), ones)
    f_out[...] = lax.fori_loop(0, rounds, round_body, carry)[3]


def per_device(sizes, v, counts, spin, flags, parity, displacement, heat):
    slots = v.shape[1]
    ex, ey, nz = counts.shape
    steps = spin.shape[0]
    rounds = steps // 2
    bonds = (max(ex, ey) + 1) // 2
    assert ex % 2 == 1 and ey % 2 == 1 and ex == ey
    f32, i32 = jnp.float32, jnp.int32
    anywhere = pl.BlockSpec(memory_space=pltpu.HBM)
    scalar = pl.BlockSpec(memory_space=pltpu.SMEM)
    vector = pl.BlockSpec(memory_space=pltpu.VMEM)
    dma = pltpu.SemaphoreType.DMA
    x, f = pl.pallas_call(
        functools.partial(kernel, sizes),
        out_shape=(
            jax.ShapeDtypeStruct(v.shape, f32),
            jax.ShapeDtypeStruct((1, nz), f32),
        ),
        in_specs=[anywhere] * 4 + [scalar] * 3,
        out_specs=(vector, vector),
        scratch_shapes=[
            pltpu.VMEM(v.shape, f32),
            pltpu.VMEM(spin.shape, i32),
            pltpu.VMEM((rounds, ex + 2, ey, nz), i32),
            pltpu.VMEM((rounds, ey + 2, ex, nz), i32),
            pltpu.VMEM((rounds, ex, ey, nz), i32),
            pltpu.VMEM((ex + 2, ey, nz), i32),
            pltpu.VMEM((ey + 2, ex, nz), i32),
            pltpu.VMEM((ex + 2, ey, nz), f32),
            pltpu.VMEM((ey + 2, ex, nz), f32),
            pltpu.VMEM((ex, ey, nz), f32),
            pltpu.VMEM((ex, ey, nz), f32),
            pltpu.VMEM((ex + 2, ey, nz), f32),
            pltpu.VMEM((ey + 2, ex, nz), f32),
            pltpu.VMEM((ex + 1, ey, nz), f32),
            pltpu.VMEM((ey + 1, ex, nz), f32),
            pltpu.VMEM((bonds, ey, nz), f32),
            pltpu.VMEM((bonds, ey, nz), f32),
            pltpu.VMEM((bonds, ey, nz), f32),
            pltpu.VMEM((2, sizes[1], 2, nz), f32),
            pltpu.VMEM((2, sizes[0], 2, nz), f32),
            dma((7,)),
            dma((12,)),
            dma((12,)),
            dma((2,)),
            dma((2,)),
            dma((2,)),
            dma((2,)),
        ],
        compiler_params=pltpu.CompilerParams(
            collective_id=0, has_side_effects=True, vmem_limit_bytes=40 * 2**20
        ),
    )(
        v,
        counts,
        spin,
        flags.reshape((rounds, 2) + flags.shape[1:]),
        parity,
        displacement,
        heat,
    )
    return x * f[0]


def solution(mesh):
    sizes = (mesh.shape["bx"], mesh.shape["by"])
    cells = P(None, "bx", "by", None)
    return jax.shard_map(
        functools.partial(per_device, sizes),
        mesh=mesh,
        in_specs=(
            P(None, None, "bx", "by", None),
            P("bx", "by", None),
            cells,
            cells,
            P(),
            P(),
            P(),
        ),
        out_specs=P(None, None, "bx", "by", None),
        check_vma=False,
    )
```

profile of v0, /device:TPU:0, one launch (start us, length us, event | category | flops | bytes accessed | tf_op | source)
XLA Modules:
  0.0 101.8 jit_solution(17525932372985950543)
XLA Ops:
  0.0 0.0 copy-start
  0.0 1.6 %copy-done = f32[3,6,15,15,128]{4,3,2,1,0:T(8,128)S(1)} copy-done((f32[3,6,15,15,128]{4,3,2,1,0:T(8,128)S(1)}, f32[3,6,15,15,128]{4,3,2,1,0:T(8,128)}, u32[]{:S(2)}) %copy-start) | copy-done | bytes 2073624
  1.6 0.0 copy-start.1
  1.6 1.4 %copy-done.1 = s32[12,15,15,128]{3,2,1,0:T(8,128)S(1)} copy-done((s32[12,15,15,128]{3,2,1,0:T(8,128)S(1)}, s32[12,15,15,128]{3,2,1,0:T(8,128)}, u32[]{:S(2)}) %copy-start.1) | copy-done | bytes 1382424
  3.0 0.0 copy-start.2
  3.0 1.4 %copy-done.2 = s32[12,15,15,128]{3,2,1,0:T(8,128)S(1)} copy-done((s32[12,15,15,128]{3,2,1,0:T(8,128)S(1)}, s32[12,15,15,128]{3,2,1,0:T(8,128)}, u32[]{:S(2)}) %copy-start.2) | copy-done | bytes 1382424
  4.4 0.0 copy-start.3
  4.4 0.9 copy-done.3
  5.3 0.0 copy-start.4
  5.3 0.7 copy-done.4
  5.9 0.0 copy-start.5
  5.9 0.7 copy-done.5
  6.6 0.0 copy-start.6
  6.6 0.7 copy-done.6
  7.2 93.1 %shard_map.73 = (f32[3,6,15,15,128]{4,3,2,1,0:T(8,128)S(1)}, f32[1,128]{1,0:T(1,128)S(1)}) custom-call(f32[3,6,15,15,128]{4,3,2,1,0:T(8,128)S(1)} %copy-done, s32[15,15,128]{2,1,0:T(8,128)S(1)} %copy-done.3, s32[12,15,15,128]{3,2,1,0:T(8,128)S(1)} %copy-done.1, s32[6,2,15,15,128]{4,3,2,1,0:T(8,128)S(1)} %bitcast.2, s32[12]{0:T(128)S(1)} %copy-done.4, ...), custom_call_target="tpu_custom_call" | custom-call | tf_op jit(solution)/shard_map/pallas_call | solution.py:376
  100.3 1.5 %broadcast_multiply_fusion = f32[3,6,15,15,128]{4,3,2,1,0:T(8,128)} fusion(f32[3,6,15,15,128]{4,3,2,1,0:T(8,128)S(1)} %get-tuple-element.7, f32[128]{0:T(128)S(1)} %bitcast.3), kind=kLoop, calls=%fused_computation | loop fusion | flops 518400 | bytes 4147712 | tf_op jit(solution)/shard_map/mul | solution.py:425
Async XLA Ops:
  0.0 1.6 %copy-start = (f32[3,6,15,15,128]{4,3,2,1,0:T(8,128)S(1)}, f32[3,6,15,15,128]{4,3,2,1,0:T(8,128)}, u32[]{:S(2)}) copy-start(f32[3,6,15,15,128]{4,3,2,1,0:T(8,128)} %v_hbm.1) | copy-start | bytes 6220804
  1.6 1.4 %copy-start.1 = (s32[12,15,15,128]{3,2,1,0:T(8,128)S(1)}, s32[12,15,15,128]{3,2,1,0:T(8,128)}, u32[]{:S(2)}) copy-start(s32[12,15,15,128]{3,2,1,0:T(8,128)} %spin_hbm.1) | copy-start | bytes 4147204
  3.0 1.4 %copy-start.2 = (s32[12,15,15,128]{3,2,1,0:T(8,128)S(1)}, s32[12,15,15,128]{3,2,1,0:T(8,128)}, u32[]{:S(2)}) copy-start(s32[12,15,15,128]{3,2,1,0:T(8,128)} %param.10) | copy-start | bytes 4147204
  4.4 0.9 copy-start.3
  5.3 0.7 copy-start.4
  5.9 0.7 copy-start.5
  6.6 0.7 copy-start.6
where the time goes:
time: 102 us
  Pallas kernels  93.1 us (91%)
  local copies, waits for them, and re-layouts  7.23 us (7%)
  other arithmetic  1.53 us (2%)
    pallas_call x1, Pallas kernels, per_device(): pl.pallas_call(functools.partial(kernel, sizes), out_shape=(jax.ShapeDtyp...  93.1 us
    unnamed x14, local copies, waits for them, and re-layouts  7.23 us

commit v1 on v0

--- a/solution.py
+++ b/solution.py
@@ -32,11 +32,14 @@
     count_hbm,
     spin_hbm,
     flag_hbm,
+    parity_hbm,
+    displacement_hbm,
+    heat_hbm,
+    x_out,
+    f_out,
     parity,
     displacement,
     heat,
-    x_out,
-    f_out,
     w,
     spin,
     flag_x,
@@ -55,15 +58,12 @@
     closing,
     coupling,
     transfer,
-    rows_by,
-    rows_bx,
+    rows,
     load_sem,
     halo_send,
     halo_recv,
-    by_send,
-    by_recv,
-    bx_send,
-    bx_recv,
+    row_send,
+    row_recv,
 ):
     n = sizes
     slots = v_hbm.shape[1]
@@ -73,6 +73,10 @@
     me = (lax.axis_index("bx"), lax.axis_index("by"))
     above = tuple(lax.rem(me[a] + 1, n[a]) for a in range(2))
     below = tuple(lax.rem(me[a] + n[a] - 1, n[a]) for a in range(2))
+    my_row = me[0] * n[1] + me[1]
+    offsets = [(i, j) for i in range(n[0]) for j in range(n[1]) if i or j]
+    offsets.sort(key=lambda o: -(min(o[0], n[0] - o[0]) + min(o[1], n[1] - o[1])))
+    peers = [(lax.rem(me[0] + i, n[0]), lax.rem(me[1] + j, n[1])) for i, j in offsets]
     flag = (flag_x, flag_y)
     count = (count_x, count_y)
     mom = (p_x, p_y)
@@ -84,18 +88,20 @@
     load_fx = pltpu.make_async_copy(flag_hbm.at[:, 0], flag_x.at[:, pl.ds(1, ex)], load_sem.at[4])
     load_fy = pltpu.make_async_copy(flag_hbm.at[:, 1], flag_raw, load_sem.at[5])
     load_spin = pltpu.make_async_copy(spin_hbm, spin, load_sem.at[6])
+    load_scalars = [
+        pltpu.make_async_copy(source, target, load_sem.at[7 + i])
+        for i, (source, target) in enumerate(
+            ((parity_hbm, parity), (displacement_hbm, displacement), (heat_hbm, heat))
+        )
+    ]
+    for copy in load_scalars:
+        copy.start()
     for copy in (load_count, load_v[0], load_fx, load_v[1], load_fy, load_v[2], load_spin):
         copy.start()
 
     barrier = pltpu.get_barrier_semaphore()
-    for a in range(2):
-        for step in range(1, n[a]):
-            pl.semaphore_signal(
-                barrier,
-                inc=1,
-                device_id={AXES[a]: lax.rem(me[a] + step, n[a])},
-                device_id_type=MESH,
-            )
+    for peer in peers:
+        pl.semaphore_signal(barrier, inc=1, device_id=peer, device_id_type=MESH)
 
     def halo(view, a, kind):
         k = 2 * (2 * kind + a)
@@ -157,7 +163,7 @@
         number = number + count_x[i].astype(jnp.float32)
     load_v[0].wait()
     thermal_0, energy_x = split_component(0, p_x, 1)
-    pl.semaphore_wait(barrier, n[0] + n[1] - 2)
+    pl.semaphore_wait(barrier, n[0] * n[1] - 1)
     start(halo_p[0])
     start(halo_c[0])
     load_fx.wait()
@@ -225,27 +231,27 @@
 
         lax.fori_loop(0, ex, plane, 0)
 
-    def exchange(rows, a, slot, send_sem, recv_sem):
+    def exchange(a):
         return [
             pltpu.make_async_remote_copy(
-                src_ref=rows.at[slot, me[a]],
-                dst_ref=rows.at[slot, me[a]],
-                send_sem=send_sem,
-                recv_sem=recv_sem,
-                device_id={AXES[a]: lax.rem(me[a] + step, n[a])},
+                src_ref=rows.at[a, my_row],
+                dst_ref=rows.at[a, my_row],
+                send_sem=row_send.at[a],
+                recv_sem=row_recv.at[a],
+                device_id=peer,
                 device_id_type=MESH,
             )
-            for step in range(1, n[a])
+            for peer in peers
         ]
 
-    def await_rows(rows, a, slot, send_sem, recv_sem):
-        view = rows.at[slot, pl.ds(0, n[a] - 1)]
+    def await_rows(a):
+        view = rows.at[a, pl.ds(0, n[0] * n[1] - 1)]
         whole = pltpu.make_async_remote_copy(
             src_ref=view,
             dst_ref=view,
-            send_sem=send_sem,
-            recv_sem=recv_sem,
-            device_id={AXES[a]: above[a]},
+            send_sem=row_send.at[a],
+            recv_sem=row_recv.at[a],
+            device_id=peers[0],
             device_id_type=MESH,
         )
         whole.wait_recv()
@@ -268,6 +274,8 @@
         return column_sum(tree_sum(energy))
 
     load_spin.wait()
+    for copy in load_scalars:
+        copy.wait()
     reduced_masses(0)
     finish(halo_f[0])
     prepare(0, 0, 0, 0)
@@ -279,8 +287,8 @@
         b = 1 - a
         new_energy = collide(a, t, scales[a])
         partial = new_energy + energies[b] + energies[2]
-        rows_by[a, me[1]] = jnp.concatenate([partial, number_row], axis=0)
-        start(exchange(rows_by, 1, a, by_send.at[a], by_recv.at[a]))
+        rows[a, my_row] = jnp.concatenate([partial, number_row], axis=0)
+        start(exchange(a))
         if a == 0:
 
             @pl.when(r > 0)
@@ -301,9 +309,6 @@
                 reduced_masses(1)
                 finish(halo_f[1])
 
-        await_rows(rows_by, 1, a, by_send.at[a], by_recv.at[a])
-        rows_bx[a, me[0]] = tree_sum([rows_by[a, i] for i in range(n[1])])
-        start(exchange(rows_bx, 0, a, bx_send.at[a], bx_recv.at[a]))
         new_shift = lax.rem(shift + displacement[t], nz)
         if a == 0:
             prepare(1, r, t + 1, new_shift)
@@ -317,8 +322,8 @@
             def _():
                 last_hook(scales, new_shift)
 
-        await_rows(rows_bx, 0, a, bx_send.at[a], bx_recv.at[a])
-        sums = tree_sum([rows_bx[a, i] for i in range(n[0])])
+        await_rows(a)
+        sums = tree_sum([rows[a, i] for i in range(n[0] * n[1])])
         sums = jnp.sum(sums, axis=1, keepdims=True)
         square = 3.0 * heat[t] * sums[1:2] / (sums[0:1] + EPSILON)
         square = jnp.broadcast_to(square, (1, nz))
@@ -370,7 +375,6 @@
     assert ex % 2 == 1 and ey % 2 == 1 and ex == ey
     f32, i32 = jnp.float32, jnp.int32
     anywhere = pl.BlockSpec(memory_space=pltpu.HBM)
-    scalar = pl.BlockSpec(memory_space=pltpu.SMEM)
     vector = pl.BlockSpec(memory_space=pltpu.VMEM)
     dma = pltpu.SemaphoreType.DMA
     x, f = pl.pallas_call(
@@ -379,9 +383,12 @@
             jax.ShapeDtypeStruct(v.shape, f32),
             jax.ShapeDtypeStruct((1, nz), f32),
         ),
-        in_specs=[anywhere] * 4 + [scalar] * 3,
+        in_specs=[anywhere] * 7,
         out_specs=(vector, vector),
         scratch_shapes=[
+            pltpu.SMEM(parity.shape, i32),
+            pltpu.SMEM(displacement.shape, i32),
+            pltpu.SMEM(heat.shape, f32),
             pltpu.VMEM(v.shape, f32),
             pltpu.VMEM(spin.shape, i32),
             pltpu.VMEM((rounds, ex + 2, ey, nz), i32),
@@ -400,13 +407,10 @@
             pltpu.VMEM((bonds, ey, nz), f32),
             pltpu.VMEM((bonds, ey, nz), f32),
             pltpu.VMEM((bonds, ey, nz), f32),
-            pltpu.VMEM((2, sizes[1], 2, nz), f32),
-            pltpu.VMEM((2, sizes[0], 2, nz), f32),
-            dma((7,)),
+            pltpu.VMEM((2, sizes[0] * sizes[1], 2, nz), f32),
+            dma((10,)),
             dma((12,)),
             dma((12,)),
-            dma((2,)),
-            dma((2,)),
             dma((2,)),
             dma((2,)),
         ],
@@ -414,13 +418,18 @@
             collective_id=0, has_side_effects=True, vmem_limit_bytes=40 * 2**20
         ),
     )(
-        v,
-        counts,
-        spin,
-        flags.reshape((rounds, 2) + flags.shape[1:]),
-        parity,
-        displacement,
-        heat,
+        *(
+            pltpu.with_memory_space_constraint(value, pltpu.HBM)
+            for value in (
+                v,
+                counts,
+                spin,
+                flags.reshape((rounds, 2) + flags.shape[1:]),
+                parity,
+                displacement,
+                heat,
+            )
+        )
     )
     return x * f[0]
 

time: 102 us -> 70.7 us (0.69)
  Pallas kernels: 93.1 us -> 69 us
  local copies, waits for them, and re-layouts: 7.23 us -> 0 us
    pallas_call x1, Pallas kernels: 93.1 us -> 69 us  [per_device(): pl.pallas_call(functools.partial(kernel, sizes), out_shape=(jax.ShapeDtyp...]
    unnamed x14 -> x0, local copies, waits for them, and re-layouts: 7.23 us -> none
where the time goes in v1:
time: 70.7 us; the launch traced here: 70.5 us
  Pallas kernels  69 us (98%)
  other arithmetic  1.55 us (2%)
    pallas_call x1, Pallas kernels, per_device(): pl.pallas_call(functools.partial(kernel, sizes), out_shape=(jax.ShapeDtyp...  69 us
    mul x1, other arithmetic, per_device(): return x * f[0]  1.55 us

profile of v1, /device:TPU:0, one launch (start us, length us, event | category | flops | bytes accessed | tf_op | source)
XLA Modules:
  0.0 70.5 jit_solution(12760999571057283005)
XLA Ops:
  0.0 69.0 %shard_map.73 = (f32[3,6,15,15,128]{4,3,2,1,0:T(8,128)S(1)}, f32[1,128]{1,0:T(1,128)S(1)}) custom-call(f32[3,6,15,15,128]{4,3,2,1,0:T(8,128)} %v_hbm.1, s32[15,15,128]{2,1,0:T(8,128)} %count_hbm.1, s32[12,15,15,128]{3,2,1,0:T(8,128)} %spin_hbm.1, s32[6,2,15,15,128]{4,3,2,1,0:T(8,128)} %bitcast.3, s32[12]{0:T(128)} %parity_hbm.1, s32[12]{0:T(128)} %displacement_hbm.1, ...), custom_call_target="tpu_custom_call" | custom-call | tf_op jit(solution)/shard_map/pallas_call | solution.py:380
  69.0 1.5 %broadcast_multiply_fusion = f32[3,6,15,15,128]{4,3,2,1,0:T(8,128)} fusion(f32[3,6,15,15,128]{4,3,2,1,0:T(8,128)S(1)} %get-tuple-element.7, f32[128]{0:T(128)S(1)} %bitcast.2), kind=kLoop, calls=%fused_computation | loop fusion | flops 518400 | bytes 4147712 | tf_op jit(solution)/shard_map/mul | solution.py:434

commit v2 on v1

--- a/solution.py
+++ b/solution.py
@@ -64,6 +64,10 @@
     halo_recv,
     row_send,
     row_recv,
+    numbers,
+    number_send,
+    number_recv,
+    total,
 ):
     n = sizes
     slots = v_hbm.shape[1]
@@ -139,6 +143,32 @@
     def inverse(counts):
         return 1.0 / jnp.maximum(counts.astype(jnp.float32), 1.0)
 
+    def exchange(a, rows=rows, row_send=row_send, row_recv=row_recv):
+        return [
+            pltpu.make_async_remote_copy(
+                src_ref=rows.at[a, my_row],
+                dst_ref=rows.at[a, my_row],
+                send_sem=row_send.at[a],
+                recv_sem=row_recv.at[a],
+                device_id=peer,
+                device_id_type=MESH,
+            )
+            for peer in peers
+        ]
+
+    def await_rows(a, rows=rows, row_send=row_send, row_recv=row_recv):
+        view = rows.at[a, pl.ds(0, n[0] * n[1] - 1)]
+        whole = pltpu.make_async_remote_copy(
+            src_ref=view,
+            dst_ref=view,
+            send_sem=row_send.at[a],
+            recv_sem=row_recv.at[a],
+            device_id=peers[0],
+            device_id_type=MESH,
+        )
+        whole.wait_recv()
+        whole.wait_send()
+
     def split_component(c, target, offset):
         def plane(i, acc):
             counts = count_x[i + 1]
@@ -168,6 +198,8 @@
     start(halo_c[0])
     load_fx.wait()
     start(halo_f[0])
+    numbers[0, my_row] = column_sum(number)
+    start(exchange(0, numbers, number_send, number_recv))
     load_v[1].wait()
     thermal_1, energy_y = split_component(1, p_tmp, 0)
     for y in range(ey):
@@ -230,32 +262,6 @@
             return carry
 
         lax.fori_loop(0, ex, plane, 0)
-
-    def exchange(a):
-        return [
-            pltpu.make_async_remote_copy(
-                src_ref=rows.at[a, my_row],
-                dst_ref=rows.at[a, my_row],
-                send_sem=row_send.at[a],
-                recv_sem=row_recv.at[a],
-                device_id=peer,
-                device_id_type=MESH,
-            )
-            for peer in peers
-        ]
-
-    def await_rows(a):
-        view = rows.at[a, pl.ds(0, n[0] * n[1] - 1)]
-        whole = pltpu.make_async_remote_copy(
-            src_ref=view,
-            dst_ref=view,
-            send_sem=row_send.at[a],
-            recv_sem=row_recv.at[a],
-            device_id=peers[0],
-            device_id_type=MESH,
-        )
-        whole.wait_recv()
-        whole.wait_send()
 
     def collide(a, t, scale):
         p = offset_of(a, t)
@@ -279,7 +285,6 @@
     reduced_masses(0)
     finish(halo_f[0])
     prepare(0, 0, 0, 0)
-    number_row = column_sum(number)
     ones = jnp.ones((1, nz), jnp.float32)
 
     def step(a, r, scales, energies, shift, last_hook):
@@ -287,7 +292,7 @@
         b = 1 - a
         new_energy = collide(a, t, scales[a])
         partial = new_energy + energies[b] + energies[2]
-        rows[a, my_row] = jnp.concatenate([partial, number_row], axis=0)
+        rows[a, my_row] = partial
         start(exchange(a))
         if a == 0:
 
@@ -308,6 +313,10 @@
             def _():
                 reduced_masses(1)
                 finish(halo_f[1])
+                await_rows(0, numbers, number_send, number_recv)
+                everyone = tree_sum([numbers[0, i] for i in range(n[0] * n[1])])
+                everyone = jnp.sum(everyone, axis=1, keepdims=True)
+                total[...] = jnp.broadcast_to(everyone, (1, nz))
 
         new_shift = lax.rem(shift + displacement[t], nz)
         if a == 0:
@@ -325,8 +334,8 @@
         await_rows(a)
         sums = tree_sum([rows[a, i] for i in range(n[0] * n[1])])
         sums = jnp.sum(sums, axis=1, keepdims=True)
-        square = 3.0 * heat[t] * sums[1:2] / (sums[0:1] + EPSILON)
-        square = jnp.broadcast_to(square, (1, nz))
+        kinetic = jnp.broadcast_to(sums, (1, nz))
+        square = (3.0 * heat[t]) * total[...] / (kinetic + EPSILON)
         f = jnp.sqrt(square)
         kept = scales[b] * f
         scales = (f, kept, scales[2] * f) if a == 0 else (kept, f, scales[2] * f)
@@ -407,12 +416,16 @@
             pltpu.VMEM((bonds, ey, nz), f32),
             pltpu.VMEM((bonds, ey, nz), f32),
             pltpu.VMEM((bonds, ey, nz), f32),
-            pltpu.VMEM((2, sizes[0] * sizes[1], 2, nz), f32),
+            pltpu.VMEM((2, sizes[0] * sizes[1], 1, nz), f32),
             dma((10,)),
             dma((12,)),
             dma((12,)),
             dma((2,)),
             dma((2,)),
+            pltpu.VMEM((1, sizes[0] * sizes[1], 1, nz), f32),
+            dma((1,)),
+            dma((1,)),
+            pltpu.VMEM((1, nz), f32),
         ],
         compiler_params=pltpu.CompilerParams(
             collective_id=0, has_side_effects=True, vmem_limit_bytes=40 * 2**20

time: 70.7 us -> 69 us (0.976)
  Pallas kernels: 69 us -> 67.3 us
    pallas_call x1, Pallas kernels: 69 us -> 67.3 us  [per_device(): pl.pallas_call(functools.partial(kernel, sizes), out_shape=(jax.ShapeDtyp...]
where the time goes in v2:
time: 69 us; the launch traced here: 68.9 us
  Pallas kernels  67.3 us (98%)
  other arithmetic  1.55 us (2%)
    pallas_call x1, Pallas kernels, per_device(): pl.pallas_call(functools.partial(kernel, sizes), out_shape=(jax.ShapeDtyp...  67.3 us
    mul x1, other arithmetic, per_device(): return x * f[0]  1.55 us

profile of v2, /device:TPU:0, one launch (start us, length us, event | category | flops | bytes accessed | tf_op | source)
XLA Modules:
  0.0 68.9 jit_solution(14405794901272699640)
XLA Ops:
  0.0 67.3 %shard_map.73 = (f32[3,6,15,15,128]{4,3,2,1,0:T(8,128)S(1)}, f32[1,128]{1,0:T(1,128)S(1)}) custom-call(f32[3,6,15,15,128]{4,3,2,1,0:T(8,128)} %v_hbm.1, s32[15,15,128]{2,1,0:T(8,128)} %count_hbm.1, s32[12,15,15,128]{3,2,1,0:T(8,128)} %spin_hbm.1, s32[6,2,15,15,128]{4,3,2,1,0:T(8,128)} %bitcast.3, s32[12]{0:T(128)} %parity_hbm.1, s32[12]{0:T(128)} %displacement_hbm.1, ...), custom_call_target="tpu_custom_call" | custom-call | tf_op jit(solution)/shard_map/pallas_call | solution.py:389
  67.3 1.5 %broadcast_multiply_fusion = f32[3,6,15,15,128]{4,3,2,1,0:T(8,128)} fusion(f32[3,6,15,15,128]{4,3,2,1,0:T(8,128)S(1)} %get-tuple-element.7, f32[128]{0:T(128)S(1)} %bitcast.2), kind=kLoop, calls=%fused_computation | loop fusion | flops 518400 | bytes 4147712 | tf_op jit(solution)/shard_map/mul | solution.py:447

commit v3 on v2

--- a/solution.py
+++ b/solution.py
@@ -78,9 +78,25 @@
     above = tuple(lax.rem(me[a] + 1, n[a]) for a in range(2))
     below = tuple(lax.rem(me[a] + n[a] - 1, n[a]) for a in range(2))
     my_row = me[0] * n[1] + me[1]
-    offsets = [(i, j) for i in range(n[0]) for j in range(n[1]) if i or j]
-    offsets.sort(key=lambda o: -(min(o[0], n[0] - o[0]) + min(o[1], n[1] - o[1])))
-    peers = [(lax.rem(me[0] + i, n[0]), lax.rem(me[1] + j, n[1])) for i, j in offsets]
+    columns = [me[0]]
+    if n[0] % 2 == 0:
+        half = n[0] // 2
+        for i in range(half):
+            for k in range(2):
+                if i or k:
+                    columns.append(
+                        2 * lax.rem(me[0] // 2 + i, half) + lax.rem(lax.rem(me[0], 2) + k, 2)
+                    )
+    else:
+        columns += [lax.rem(me[0] + i, n[0]) for i in range(1, n[0])]
+    low_half = (2 * me[1]) // n[1] == 0
+    peers = []
+    for k in range(n[1] - 1):
+        down = jnp.where(n[1] - 1 - k > me[1], n[1] - 1 - k, n[1] - 2 - k)
+        up = jnp.where(k < me[1], k, k + 1)
+        row = jnp.where(low_half, down, up)
+        peers += [(column, row) for column in reversed(columns)]
+    peers += [(column, me[1]) for column in reversed(columns[1:])]
     flag = (flag_x, flag_y)
     count = (count_x, count_y)
     mom = (p_x, p_y)
@@ -335,8 +351,8 @@
         sums = tree_sum([rows[a, i] for i in range(n[0] * n[1])])
         sums = jnp.sum(sums, axis=1, keepdims=True)
         kinetic = jnp.broadcast_to(sums, (1, nz))
-        square = (3.0 * heat[t]) * total[...] / (kinetic + EPSILON)
-        f = jnp.sqrt(square)
+        f = jnp.sqrt((3.0 * heat[t]) * total[...]) * lax.rsqrt(kinetic + EPSILON)
+        square = f * f
         kept = scales[b] * f
         scales = (f, kept, scales[2] * f) if a == 0 else (kept, f, scales[2] * f)
         moved = new_energy * square

time: 69 us -> 67.8 us (0.983)
  Pallas kernels: 67.3 us -> 66.1 us
    pallas_call x1, Pallas kernels: 67.3 us -> 66.1 us  [per_device(): pl.pallas_call(functools.partial(kernel, sizes), out_shape=(jax.ShapeDtyp...]
where the time goes in v3:
time: 67.8 us; the launch traced here: 67.6 us
  Pallas kernels  66.1 us (97%)
  other arithmetic  1.55 us (2%)
    pallas_call x1, Pallas kernels, per_device(): pl.pallas_call(functools.partial(kernel, sizes), out_shape=(jax.ShapeDtyp...  66.1 us
    mul x1, other arithmetic, per_device(): return x * f[0]  1.55 us

profile of v3, /device:TPU:0, one launch (start us, length us, event | category | flops | bytes accessed | tf_op | source)
XLA Modules:
  0.0 67.6 jit_solution(1867218775034369262)
XLA Ops:
  0.0 66.1 %shard_map.73 = (f32[3,6,15,15,128]{4,3,2,1,0:T(8,128)S(1)}, f32[1,128]{1,0:T(1,128)S(1)}) custom-call(f32[3,6,15,15,128]{4,3,2,1,0:T(8,128)} %v_hbm.1, s32[15,15,128]{2,1,0:T(8,128)} %count_hbm.1, s32[12,15,15,128]{3,2,1,0:T(8,128)} %spin_hbm.1, s32[6,2,15,15,128]{4,3,2,1,0:T(8,128)} %bitcast.3, s32[12]{0:T(128)} %parity_hbm.1, s32[12]{0:T(128)} %displacement_hbm.1, ...), custom_call_target="tpu_custom_call" | custom-call | tf_op jit(solution)/shard_map/pallas_call | solution.py:405
  66.1 1.5 %broadcast_multiply_fusion = f32[3,6,15,15,128]{4,3,2,1,0:T(8,128)} fusion(f32[3,6,15,15,128]{4,3,2,1,0:T(8,128)S(1)} %get-tuple-element.7, f32[128]{0:T(128)S(1)} %bitcast.2), kind=kLoop, calls=%fused_computation | loop fusion | flops 518400 | bytes 4147712 | tf_op jit(solution)/shard_map/mul | solution.py:463

commit v4 on v3

--- a/solution.py
+++ b/solution.py
@@ -146,7 +146,10 @@
 
     halo_p = [halo(lambda i, a=a: mom[a].at[i], a, 0) for a in range(2)]
     halo_c = [halo(lambda i, a=a: count[a].at[i], a, 1) for a in range(2)]
-    halo_f = [halo(lambda i, a=a: flag[a].at[:, i], a, 2) for a in range(2)]
+    halo_f = [halo(lambda i, a=a: flag[a].at[0, i], a, 2) for a in range(2)]
+    halo_rest = [
+        halo(lambda i, a=a: flag[a].at[pl.ds(1, rounds - 1), i], a, 3) for a in range(2)
+    ]
 
     def start(copies):
         for copy in copies:
@@ -258,7 +261,8 @@
             closing[j] = jnp.maximum(
                 mom[a][low] * iq[a][low] - mom[a][high] * iq[a][high], 0.0
             )
-            bits = jnp.maximum(flag[a][r, low], flag[a][r, high]).astype(jnp.float32)
+            outer = jnp.where(p == 0, flag[a][r, 2 * j + 2], flag[a][r, 2 * j])
+            bits = jnp.maximum(flag[a][r, 2 * j + 1], outer).astype(jnp.float32)
             coupling[j] = pltpu.roll(bits, back, 1) * rr[a][low]
 
     def rotate(t, shift):
@@ -327,6 +331,8 @@
 
             @pl.when(r == 0)
             def _():
+                start(halo_rest[0])
+                start(halo_rest[1])
                 reduced_masses(1)
                 finish(halo_f[1])
                 await_rows(0, numbers, number_send, number_recv)
@@ -339,6 +345,11 @@
             prepare(1, r, t + 1, new_shift)
         else:
 
+            @pl.when(r == 0)
+            def _():
+                finish(halo_rest[0])
+                finish(halo_rest[1])
+
             @pl.when(r < rounds - 1)
             def _():
                 prepare(0, r + 1, t + 1, new_shift)
@@ -347,11 +358,12 @@
             def _():
                 last_hook(scales, new_shift)
 
+        root = jnp.sqrt((3.0 * heat[t]) * total[...])
         await_rows(a)
         sums = tree_sum([rows[a, i] for i in range(n[0] * n[1])])
         sums = jnp.sum(sums, axis=1, keepdims=True)
         kinetic = jnp.broadcast_to(sums, (1, nz))
-        f = jnp.sqrt((3.0 * heat[t]) * total[...]) * lax.rsqrt(kinetic + EPSILON)
+        f = root * lax.rsqrt(kinetic + EPSILON)
         square = f * f
         kept = scales[b] * f
         scales = (f, kept, scales[2] * f) if a == 0 else (kept, f, scales[2] * f)
@@ -434,8 +446,8 @@
             pltpu.VMEM((bonds, ey, nz), f32),
             pltpu.VMEM((2, sizes[0] * sizes[1], 1, nz), f32),
             dma((10,)),
-            dma((12,)),
-            dma((12,)),
+            dma((16,)),
+            dma((16,)),
             dma((2,)),
             dma((2,)),
             pltpu.VMEM((1, sizes[0] * sizes[1], 1, nz), f32),

time: 67.8 us -> 66.3 us (0.978)
  Pallas kernels: 66.1 us -> 64.6 us
    pallas_call x1, Pallas kernels: 66.1 us -> 64.6 us  [per_device(): pl.pallas_call(functools.partial(kernel, sizes), out_shape=(jax.ShapeDtyp...]
where the time goes in v4:
time: 66.3 us; the launch traced here: 66.2 us
  Pallas kernels  64.6 us (97%)
  other arithmetic  1.55 us (2%)
    pallas_call x1, Pallas kernels, per_device(): pl.pallas_call(functools.partial(kernel, sizes), out_shape=(jax.ShapeDtyp...  64.6 us
    mul x1, other arithmetic, per_device(): return x * f[0]  1.55 us

profile of v4, /device:TPU:0, one launch (start us, length us, event | category | flops | bytes accessed | tf_op | source)
XLA Modules:
  0.0 66.2 jit_solution(10576909032980777362)
XLA Ops:
  0.0 64.6 %shard_map.73 = (f32[3,6,15,15,128]{4,3,2,1,0:T(8,128)S(1)}, f32[1,128]{1,0:T(1,128)S(1)}) custom-call(f32[3,6,15,15,128]{4,3,2,1,0:T(8,128)} %v_hbm.1, s32[15,15,128]{2,1,0:T(8,128)} %count_hbm.1, s32[12,15,15,128]{3,2,1,0:T(8,128)} %spin_hbm.1, s32[6,2,15,15,128]{4,3,2,1,0:T(8,128)} %bitcast.3, s32[12]{0:T(128)} %parity_hbm.1, s32[12]{0:T(128)} %displacement_hbm.1, ...), custom_call_target="tpu_custom_call" | custom-call | tf_op jit(solution)/shard_map/pallas_call | solution.py:417
  64.6 1.5 %broadcast_multiply_fusion = f32[3,6,15,15,128]{4,3,2,1,0:T(8,128)} fusion(f32[3,6,15,15,128]{4,3,2,1,0:T(8,128)S(1)} %get-tuple-element.7, f32[128]{0:T(128)S(1)} %bitcast.2), kind=kLoop, calls=%fused_computation | loop fusion | flops 518400 | bytes 4147712 | tf_op jit(solution)/shard_map/mul | solution.py:475
